TPU v7x, 32 devices: a whole 2x2x4 slice. The times are simulated.
32 devices in a mesh: groups: 2 (over y), shard: 4 (over z), dp: 2 (over x), tok: 2 (over core).
Axes of the slice: x: 2, y: 2, z: 4, core: 2. Of those that a mesh axis runs over, the one named last changes fastest.
Arguments:
- tokens: bfloat16 [2048, 4096], P(('groups', 'dp', 'tok'), 'shard'), parts along dimension 0, may hold values from -6 to 6
- gate_blocks: bfloat16 [8, 16, 128, 128], P('shard'), may hold values from -0.125 to 0.125
- up_blocks: bfloat16 [8, 16, 128, 128], P('shard'), may hold values from -0.125 to 0.125
- down_blocks: bfloat16 [8, 16, 128, 128], P('shard'), may hold values from -0.25 to 0.25
- gate_rows: int32 [8, 16], P('shard'), may hold values from 0 to 31, as said below
- up_rows: int32 [8, 16], P('shard'), may hold values from 0 to 31, as said below
- down_rows: int32 [8, 16], replicated, may hold values from 0 to 31, as said below
- cotangent: bfloat16 [2048, 4096], P(('groups', 'dp', 'tok'), 'shard'), parts along dimension 0, may hold values from -6 to 6
Outputs:
- mixed: bfloat16 [2048, 4096], P(('groups', 'dp', 'tok'), 'shard'), parts along dimension 0
- tokens_grad: bfloat16 [2048, 4096], P(('groups', 'dp', 'tok'), 'shard'), parts along dimension 0
- gate_grad: bfloat16 [16, 16, 128, 128], P(('groups', 'shard'), ('dp', 'tok')), parts along dimension 0
- up_grad: bfloat16 [16, 16, 128, 128], P(('groups', 'shard'), ('dp', 'tok')), parts along dimension 0
- down_grad: bfloat16 [16, 16, 128, 128], P(('groups', 'shard'), ('dp', 'tok')), parts along dimension 0
There are 2 independent parts, one for each index of `groups`. A program takes and returns all parts, laid end to end along the dimension named above; an argument that names none is the same for every part. Nothing has to cross between parts.
Inputs may be any that keep to these rules, and one draw needn't show every extreme that they name: `gate_rows`: in every row c of the list and for every o, the entries o * 4 to (o + 1) * 4 - 1 are distinct blocks among o * 2 * 4 to (o + 1) * 2 * 4 - 1, in ascending order. `up_rows`: as for gate_rows, drawn independently. `down_rows`: as for gate_rows, drawn independently.
All inputs are finite; a program needn't handle non-finite values.
Results may differ from a plain program's by a relative error of at most 0.018.
Values may be sent and summed in bfloat16 or wider, within the bound.
No kernel may reach another device: no remote copies, remote signals or barrier semaphores. Data moves between devices by JAX's collectives and lax.ppermute only.
A program may use at most 64 MiB of HBM per device.

v0:
```python
import jax
import jax.numpy as jnp
from jax import lax
from jax.sharding import PartitionSpec as P


def body(tokens, gate_blocks, up_blocks, down_blocks, gate_rows, up_rows, down_rows, cotangent):
    shard_count = lax.axis_size("shard")
    owner_index = lax.axis_index("shard")
    token_count = tokens.shape[0]
    owned_width = tokens.shape[1]
    column_count = gate_blocks.shape[0]
    nonzero = gate_blocks.shape[1]
    block_size = gate_blocks.shape[2]
    owned_blocks = owned_width // block_size
    per_owner = nonzero // shard_count
    gathered = lax.all_gather(tokens, "shard", axis=1, tiled=True)
    row_blocks = gathered.shape[1] // block_size
    tokens3 = gathered.reshape(token_count, row_blocks, block_size)
    gate_in = jnp.take(tokens3, gate_rows, axis=1)
    up_in = jnp.take(tokens3, up_rows, axis=1)
    gate = jnp.einsum("nckb,ckbh->nch", gate_in, gate_blocks, preferred_element_type=jnp.float32)
    up = jnp.einsum("nckb,ckbh->nch", up_in, up_blocks, preferred_element_type=jnp.float32)
    hidden = (jax.nn.silu(gate) * up).astype(jnp.bfloat16)
    out_blocks = jnp.einsum(
        "nch,ckho->ncko", hidden, down_blocks, preferred_element_type=jnp.float32
    ).astype(jnp.bfloat16)
    sending = out_blocks.reshape(token_count, column_count, shard_count, per_owner * block_size)
    received = lax.all_to_all(sending, "shard", split_axis=2, concat_axis=2, tiled=True)
    received5 = received.reshape(token_count, column_count, shard_count, per_owner, block_size)
    owner_cols = lax.dynamic_slice_in_dim(down_rows, owner_index * per_owner, per_owner, 1)
    local_rows = (
        owner_cols.reshape(shard_count, column_count, per_owner) - owner_index * owned_blocks
    )
    one_hot = (
        local_rows[:, :, :, None] == jnp.arange(owned_blocks, dtype=jnp.int32)[None, None, None, :]
    ).astype(jnp.bfloat16)
    mixed_rows = jnp.einsum(
        "ncsjb,scjr->nrb", received5, one_hot, preferred_element_type=jnp.float32
    )
    mixed = mixed_rows.reshape(token_count, owned_width).astype(jnp.bfloat16)
    own_cot = cotangent.reshape(token_count, owned_blocks, block_size)
    picked = jnp.take(own_cot, local_rows.reshape(shard_count * column_count * per_owner), axis=1)
    outgoing = picked.reshape(token_count, shard_count, column_count * per_owner * block_size)
    incoming = lax.all_to_all(outgoing, "shard", split_axis=1, concat_axis=1, tiled=True)
    cot_five = incoming.reshape(token_count, shard_count, column_count, per_owner, block_size)
    cot_form = "nocjb"
    down_five = down_blocks.reshape(column_count, shard_count, per_owner, block_size, block_size)
    hidden_grad = jnp.einsum(
        cot_form + ",cojhb->nch", cot_five, down_five, preferred_element_type=jnp.float32
    )
    sigmoid_gate = jax.nn.sigmoid(gate)
    gate_act = (hidden_grad * up * sigmoid_gate * (1.0 + gate * (1.0 - sigmoid_gate))).astype(
        jnp.bfloat16
    )
    up_act = (hidden_grad * jax.nn.silu(gate)).astype(jnp.bfloat16)
    back_gate = jnp.einsum(
        "nch,ckbh->nckb", gate_act, gate_blocks, preferred_element_type=jnp.float32
    )
    back_up = jnp.einsum("nch,ckbh->nckb", up_act, up_blocks, preferred_element_type=jnp.float32)
    column_ids = jnp.arange(column_count, dtype=jnp.int32)[:, None]
    input_terms = jnp.zeros((token_count, column_count, row_blocks, block_size), jnp.float32)
    input_terms = (
        input_terms.at[:, column_ids, gate_rows]
        .add(back_gate)
        .at[:, column_ids, up_rows]
        .add(back_up)
    )
    input_narrow = input_terms.astype(jnp.bfloat16).reshape(
        token_count, column_count, shard_count, owned_width
    )
    input_arrived = lax.all_to_all(input_narrow, "shard", split_axis=2, concat_axis=2, tiled=True)
    tokens_grad = jnp.sum(input_arrived.astype(jnp.float32), axis=(1, 2)).astype(jnp.bfloat16)
    gate_term = jnp.einsum("nckb,nch->ckbh", gate_in, gate_act, preferred_element_type=jnp.float32)
    up_term = jnp.einsum("nckb,nch->ckbh", up_in, up_act, preferred_element_type=jnp.float32)
    down_term = jnp.einsum(
        cot_form + ",nch->cojhb", cot_five, hidden, preferred_element_type=jnp.float32
    )
    down_term = down_term.reshape(column_count, nonzero, block_size, block_size)
    gate_sum, up_sum, down_sum = (
        lax.psum_scatter(
            gate_term.astype(jnp.bfloat16), ("dp", "tok"), scatter_dimension=1, tiled=True
        ).astype(jnp.float32),
        lax.psum_scatter(
            up_term.astype(jnp.bfloat16), ("dp", "tok"), scatter_dimension=1, tiled=True
        ).astype(jnp.float32),
        lax.psum_scatter(
            down_term.astype(jnp.bfloat16), ("dp", "tok"), scatter_dimension=1, tiled=True
        ).astype(jnp.float32),
    )
    return (
        mixed,
        tokens_grad,
        gate_sum.astype(jnp.bfloat16),
        up_sum.astype(jnp.bfloat16),
        down_sum.astype(jnp.bfloat16),
    )


def solution(mesh):
    in_specs = (
        P(("groups", "dp", "tok"), "shard"),
        P("shard", None, None, None),
        P("shard", None, None, None),
        P("shard", None, None, None),
        P("shard", None),
        P("shard", None),
        P(),
        P(("groups", "dp", "tok"), "shard"),
    )
    out_specs = (
        P(("groups", "dp", "tok"), "shard"),
        P(("groups", "dp", "tok"), "shard"),
        P(("groups", "shard"), ("dp", "tok"), None, None),
        P(("groups", "shard"), ("dp", "tok"), None, None),
        P(("groups", "shard"), ("dp", "tok"), None, None),
    )
    return jax.shard_map(body, mesh=mesh, in_specs=in_specs, out_specs=out_specs, check_vma=False)
```

profile of v0, /device:TPU:0, one launch (start us, length us, event | category | flops | bytes accessed | tf_op | source)
XLA Modules:
  0.0 281.4 jit_solution(18129311782604778208)
XLA Ops:
  11.8 2.1 gather_fusion
  14.0 3.3 %copy.66 = bf16[256,32,128]{0,2,1:T(8,128)(2,1)S(1)} copy(bf16[256,32,128]{2,0,1:T(8,128)(2,1)} %bitcast.152) | data formatting | bytes 4194304 | tf_op jit(solution)/shard_map/jit(_take)/gather | solution.py:43
  19.1 6.5 %all-to-all-start.1 = ((bf16[256,4,1024]{0,2,1:T(8,128)(2,1)}), bf16[256,4,1024]{0,2,1:T(8,128)(2,1)}, u32[]{:S(2)}, u32[]{:S(2)}) async-start(bf16[256,4,1024]{0,2,1:T(8,128)(2,1)} %bitcast_select_fusion), calls=%async_computation.1 | async-start | bytes 4194304 | tf_op jit(solution)/shard_map/all_to_all | solution.py:45
  27.6 68.2 %all-gather.2.cloned.1.call-done = bf16[256,4096]{0,1:T(8,128)(2,1)} async-done(((bf16[256,1024]{0,1:T(8,128)(2,1)}), bf16[256,4096]{0,1:T(8,128)(2,1)}) %all-gather.2.cloned.1.call-update) | async-done | bytes 2097168 | tf_op jit(solution)/shard_map/all_gather | solution.py:17
  95.8 3.2 %copy.54 = bf16[256,32,128]{2,0,1:T(8,128)(2,1)S(1)} copy(bf16[256,32,128]{0,2,1:T(8,128)(2,1)} %bitcast.156) | data formatting | bytes 4194304 | tf_op jit(solution)/shard_map/reshape | solution.py:19
  101.1 3.9 %copy.55 = bf16[2,16,256,128]{2,3,1,0:T(8,128)(2,1)} copy(bf16[2,16,256,128]{3,2,1,0:T(8,128)(2,1)} %bitcast.150) | data formatting | bytes 4194304 | tf_op jit(solution)/shard_map/jit(_take)/gather | solution.py:20
  107.2 4.0 %copy.58 = bf16[2,16,256,128]{2,3,1,0:T(8,128)(2,1)} copy(bf16[2,16,256,128]{3,2,1,0:T(8,128)(2,1)} %bitcast.149) | data formatting | bytes 4194304 | tf_op jit(solution)/shard_map/jit(_take)/gather | solution.py:21
  111.2 2.7 convolution_bitcast_fusion.1
  119.2 3.9 %all-to-all-start = ((bf16[256,2,4,512]{0,3,1,2:T(8,128)(2,1)}), bf16[256,2,4,512]{0,3,1,2:T(8,128)(2,1)S(1)}, u32[]{:S(2)}, u32[]{:S(2)}) async-start(bf16[256,2,4,512]{0,3,1,2:T(8,128)(2,1)} %copy.61), calls=%async_computation | async-start | bytes 4194304 | tf_op jit(solution)/shard_map/all_to_all | solution.py:29
  124.5 3.9 %fusion.35 = f32[2,256,16,128]{3,1,2,0:T(8,128)} fusion(bf16[2,16,128,128]{3,2,1,0:T(8,128)(2,1)} %param.11, bf16[256,2,128]{2,0,1:T(8,128)(2,1)S(1)} %get-tuple-element.15), kind=kOutput, calls=%fused_computation.40 | convolution fusion | flops 268435456 | bytes 5373952 | tf_op jit(solution)/shard_map/nch,ckbh->nckb/dot_general | solution.py:57
  128.4 4.3 %broadcast_in_dim.45 = f32[256,2,32,128]{3,0,2,1:T(8,128)} broadcast(f32[]{:T(128)} %constant.30.clone.1), dimensions={} | broadcast | bytes 8388612 | tf_op jit(solution)/shard_map/broadcast_in_dim | solution.py:62
  132.7 10.4 %scatter_fusion = f32[256,2,32,128]{3,0,2,1:T(8,128)} fusion(f32[256,2,32,128]{3,0,2,1:T(8,128)} %broadcast_in_dim.45, s32[32]{0:T(128)S(1)} %reshape.118, f32[32,256,128]{2,1,0:T(8,128)} %bitcast.143), kind=kCustom, calls=%fused_computation.3 | custom fusion | flops 1048576 | bytes 12583168 | tf_op jit(solution)/shard_map/scatter-add | solution.py:65
  143.1 2.7 fusion.51
  145.8 10.4 %scatter_fusion.1 = f32[256,2,32,128]{3,0,2,1:T(8,128)} fusion(f32[256,2,32,128]{3,0,2,1:T(8,128)} %scatter_fusion, s32[32]{0:T(128)S(1)} %reshape.124, f32[32,256,128]{2,1,0:T(8,128)} %bitcast.144), kind=kCustom, calls=%fused_computation.4 | custom fusion | flops 1048576 | bytes 12583168 | tf_op jit(solution)/shard_map/scatter-add | solution.py:67
  156.2 6.1 %convert_element_type.59 = bf16[256,2,32,128]{3,0,2,1:T(8,128)(2,1)} convert(f32[256,2,32,128]{3,0,2,1:T(8,128)} %scatter_fusion.1) | non-fusion elementwise | flops 2097152 | bytes 12582912 | tf_op jit(solution)/shard_map/convert_element_type | solution.py:69
  162.2 6.4 %copy.69 = bf16[256,2,32,128]{0,3,2,1:T(8,128)(2,1)} copy(bf16[256,2,32,128]{3,0,2,1:T(8,128)(2,1)} %convert_element_type.59) | data formatting | bytes 8388608 | tf_op jit(solution)/shard_map/convert_element_type | solution.py:69
  168.6 4.4 %copy.70 = bf16[256,2,4,1024]{0,3,1,2:T(8,128)(2,1)} copy(bf16[256,2,4,1024]{0,3,2,1:T(8,128)(2,1)} %bitcast.146) | data formatting | bytes 8388608 | tf_op jit(solution)/shard_map/reshape | solution.py:69
  173.0 4.9 %all-to-all-start.2 = ((bf16[256,2,4,1024]{0,3,1,2:T(8,128)(2,1)}), bf16[256,2,4,1024]{0,3,1,2:T(8,128)(2,1)}, u32[]{:S(2)}, u32[]{:S(2)}) async-start(bf16[256,2,4,1024]{0,3,1,2:T(8,128)(2,1)} %copy.70), calls=%async_computation.2 | async-start | bytes 8388608 | tf_op jit(solution)/shard_map/all_to_all | solution.py:72
  178.0 3.6 %fusion.16 = bf16[2,128,4,4,128]{4,1,3,2,0:T(8,128)(2,1)} fusion(bf16[256,4,2,4,128]{0,4,3,2,1:T(8,128)(2,1)} %bitcast.29, bf16[256,2,128]{2,0,1:T(8,128)(2,1)S(1)} %get-tuple-element.16), kind=kOutput, calls=%fused_computation.20 | convolution fusion | flops 268959744 | bytes 3276800 | tf_op jit(solution)/shard_map/nocjb,nch->cojhb/dot_general | solution.py:76
  187.0 68.0 %all-reduce.6.cloned.1.call-done = (bf16[2,16,128,128]{3,2,1,0:T(8,128)(2,1)}, bf16[2,16,128,128]{3,2,1,0:T(8,128)(2,1)}, bf16[2,16,128,128]{3,2,1,0:T(8,128)(2,1)}) async-done(((bf16[2,16,128,128]{3,2,1,0:T(8,128)(2,1)}, bf16[2,16,128,128]{3,2,1,0:T(8,128)(2,1)}, bf16[2,16,128,128]{3,2,1,0:T(8,128)(2,1)}), (bf16[2,16,128,128]{3,2,1,0:T(8,128)(2,1)}, bf16[2,16,128,128]{3,2,1,0:T(8,128)(2,1)}, ...) | async-done | bytes 3145744
  258.6 3.2 %copy.63 = bf16[256,2,4,4,128]{4,2,3,0,1:T(4,128)(2,1)} copy(bf16[256,2,4,4,128]{0,4,3,1,2:T(8,128)(2,1)S(1)} %bitcast.151) | data formatting | bytes 4194304 | tf_op jit(solution)/shard_map/reshape | solution.py:30
  261.7 3.2 %fusion.19 = bf16[8,256,128]{2,0,1:T(8,128)(2,1)S(1)} fusion(bf16[256,2,4,4,128]{4,2,3,0,1:T(4,128)(2,1)} %copy.63, s32[4,2,4]{0,2,1:T(4,128)S(1)} %copy.52), kind=kOutput, calls=%fused_computation.22 | convolution fusion | flops 17039616 | bytes 2621568 | tf_op jit(solution)/shard_map/ncsjb,scjr->nrb/dot_general | solution.py:38
  265.9 4.7 %all-to-all-done.2 = bf16[256,2,4,1024]{0,3,1,2:T(8,128)(2,1)} async-done(((bf16[256,2,4,1024]{0,3,1,2:T(8,128)(2,1)}), bf16[256,2,4,1024]{0,3,1,2:T(8,128)(2,1)}, u32[]{:S(2)}, u32[]{:S(2)}) %all-to-all-start.2) | async-done | bytes 4194336 | tf_op jit(solution)/shard_map/all_to_all | solution.py:72
  270.5 3.0 %reduce_sum.12 = bf16[256,1024]{0,1:T(8,128)(2,1)S(1)} reduce(bf16[256,2,4,1024]{0,3,1,2:T(8,128)(2,1)} %all-to-all-done.2, bf16[]{:T(256)} %constant.52.clone.1), dimensions={1,2}, to_apply=%region_2.4 | reduce | flops 1835008 | bytes 4718594 | tf_op jit(solution)/shard_map/reduce_sum | solution.py:73
  (82 shorter events, 29.6 us)
Async XLA Ops:
  7.2 107.8 %copy-start = (bf16[2,16,128,128]{3,2,1,0:T(8,128)(2,1)S(1)}, bf16[2,16,128,128]{3,2,1,0:T(8,128)(2,1)}, u32[]{:S(2)}) copy-start(bf16[2,16,128,128]{3,2,1,0:T(8,128)(2,1)} %param.12) | copy-start | bytes 3145732
  7.2 88.6 %all-gather.2.cloned.1.call-start = ((), (), s32[]{:S(2)}) async-start(), calls=%async_computation.3 | async-start | bytes 2621440 | tf_op jit(solution)/shard_map/all_gather | solution.py:17
  19.1 6.5 %copy-start.10 = (s32[2,16]{1,0:T(2,128)S(1)}, s32[2,16]{1,0:T(2,128)}, u32[]{:S(2)}) copy-start(s32[2,16]{1,0:T(2,128)} %param.14) | copy-start | bytes 388
  19.1 6.6 %copy-start.11 = (s32[2,16]{1,0:T(2,128)S(1)}, s32[2,16]{1,0:T(2,128)}, u32[]{:S(2)}) copy-start(s32[2,16]{1,0:T(2,128)} %param.15) | copy-start | bytes 388
  19.1 6.7 %copy-start.2 = (bf16[2,16,128,128]{3,2,1,0:T(8,128)(2,1)S(1)}, bf16[2,16,128,128]{3,2,1,0:T(8,128)(2,1)}, u32[]{:S(2)}) copy-start(bf16[2,16,128,128]{3,2,1,0:T(8,128)(2,1)} %param.13) | copy-start | bytes 3145732
  19.1 92.1 %all-to-all-start.1 = ((bf16[256,4,1024]{0,2,1:T(8,128)(2,1)}), bf16[256,4,1024]{0,2,1:T(8,128)(2,1)}, u32[]{:S(2)}, u32[]{:S(2)}) async-start(bf16[256,4,1024]{0,2,1:T(8,128)(2,1)} %bitcast_select_fusion), calls=%async_computation.1 | async-start | bytes 4194304 | tf_op jit(solution)/shard_map/all_to_all | solution.py:45
  27.1 86.8 %copy-start.16 = (pred[2,16]{1,0:T(4,128)(4,1)}, pred[2,16]{1,0:T(4,128)(4,1)S(1)}, u32[]{:S(2)}) copy-start(pred[2,16]{1,0:T(4,128)(4,1)S(1)} %compare_and_fusion.1) | copy-start | bytes 100
  107.2 4.0 %copy-start.3 = (bf16[2,16,128,128]{3,2,1,0:T(8,128)(2,1)S(1)}, bf16[2,16,128,128]{3,2,1,0:T(8,128)(2,1)}, u32[]{:S(2)}) copy-start(bf16[2,16,128,128]{3,2,1,0:T(8,128)(2,1)} %param.13) | copy-start | bytes 3145732
  111.2 2.7 copy-start.9
  111.2 2.7 copy-start.5
  113.9 1.6 copy-start.7
  113.9 1.6 copy-start.14
  115.5 1.2 copy-start.4
  119.2 5.3 %copy-start.12 = (s32[2,16]{1,0:T(2,128)S(1)}, s32[2,16]{1,0:T(2,128)}, u32[]{:S(2)}) copy-start(s32[2,16]{1,0:T(2,128)} %param.15) | copy-start | bytes 388
  119.2 53.8 %all-to-all-start = ((bf16[256,2,4,512]{0,3,1,2:T(8,128)(2,1)}), bf16[256,2,4,512]{0,3,1,2:T(8,128)(2,1)S(1)}, u32[]{:S(2)}, u32[]{:S(2)}) async-start(bf16[256,2,4,512]{0,3,1,2:T(8,128)(2,1)} %copy.61), calls=%async_computation | async-start | bytes 4194304 | tf_op jit(solution)/shard_map/all_to_all | solution.py:29
  173.0 97.5 %all-to-all-start.2 = ((bf16[256,2,4,1024]{0,3,1,2:T(8,128)(2,1)}), bf16[256,2,4,1024]{0,3,1,2:T(8,128)(2,1)}, u32[]{:S(2)}, u32[]{:S(2)}) async-start(bf16[256,2,4,1024]{0,3,1,2:T(8,128)(2,1)} %copy.70), calls=%async_computation.2 | async-start | bytes 8388608 | tf_op jit(solution)/shard_map/all_to_all | solution.py:72
  177.9 3.7 %copy-start.17 = (pred[2,16]{1,0:T(4,128)(4,1)S(1)}, pred[2,16]{1,0:T(4,128)(4,1)}, u32[]{:S(2)}) copy-start(pred[2,16]{1,0:T(4,128)(4,1)} %copy-done.16) | copy-start | bytes 100
  177.9 77.1 %all-reduce.6.cloned.1.call-start = ((), (), s32[]{:S(2)}) async-start(), calls=%async_computation.4 | async-start | bytes 6291456
  178.0 3.6 %copy-start.6 = (bf16[2,16,256,128]{2,3,1,0:T(8,128)(2,1)S(1)}, bf16[2,16,256,128]{2,3,1,0:T(8,128)(2,1)}, u32[]{:S(2)}) copy-start(bf16[2,16,256,128]{2,3,1,0:T(8,128)(2,1)} %copy.55) | copy-start | bytes 6291460
  181.6 1.8 copy-start.8
  181.6 1.8 copy-start.15
  185.1 0.7 copy-start.13
  265.0 9.6 %copy-start.1 = (bf16[2,16,128,128]{3,2,1,0:T(8,128)(2,1)S(1)}, bf16[2,16,128,128]{3,2,1,0:T(8,128)(2,1)}, u32[]{:S(2)}) copy-start(bf16[2,16,128,128]{3,2,1,0:T(8,128)(2,1)} %param.12) | copy-start | bytes 3145732
Sparse Core Ops, SparseCore 0:
  10.1 85.5 all-gather.1
  185.3 69.7 all-reduce.5
where the time goes:
time: 283 us; the launch traced here: 281 us
  waiting for transfers between devices  141 us (50%)
  local copies, waits for them, and re-layouts  54.1 us (19%)
  other arithmetic  33.8 us (12%)
  matrix products  22.5 us (8%)
  starting transfers between devices  15.3 us (5%)
  between operations  14.9 us (5%)
    all_gather x1, waiting for transfers between devices, body(): gathered = lax.all_gather(tokens, 'shard', axis=1, tiled=True)  68.2 us
    unnamed x3, waiting for transfers between devices  68.1 us
    scatter-add x2, other arithmetic, body(): input_terms = input_terms.at[:, column_ids, gate_rows].add(back_gate).at[...  20.7 us
    unnamed x46, local copies, waits for them, and re-layouts  12 us
    all_to_all x1, starting transfers between devices, body(): lax.all_to_all(outgoing, 'shard', split_axis=1, concat_axis=1, tiled=True)  6.48 us
    convert_element_type x1, local copies, waits for them, and re-layouts, body(): input_terms.astype(jnp.bfloat16)  6.38 us
    gather x2, local copies, waits for them, and re-layouts, body(): up_in = jnp.take(tokens3, up_rows, axis=1)  6.15 us
    convert_element_type x1, other arithmetic, body(): input_terms.astype(jnp.bfloat16)  6.09 us
  transfers between devices with their start and end apart: 5, of which 3 were waited for; matrix products, arithmetic and copies ran while one was open for 34% of the time, Pallas kernels for 0%

commit v1 on v0

--- a/solution.py
+++ b/solution.py
@@ -2,6 +2,12 @@
 import jax.numpy as jnp
 from jax import lax
 from jax.sharding import PartitionSpec as P
+
+
+def laid_out(blocks, dim):
+    dims = list(blocks.shape[1:])
+    dims[dim] *= blocks.shape[0]
+    return jnp.moveaxis(blocks, 0, dim).reshape(dims)
 
 
 def body(tokens, gate_blocks, up_blocks, down_blocks, gate_rows, up_rows, down_rows, cotangent):
@@ -14,7 +20,19 @@
     block_size = gate_blocks.shape[2]
     owned_blocks = owned_width // block_size
     per_owner = nonzero // shard_count
-    gathered = lax.all_gather(tokens, "shard", axis=1, tiled=True)
+    size = lax.axis_size("shard")
+    pairs = [(i, (i + 1) % size) for i in range(size)]
+    back = [(b, a) for a, b in pairs]
+    lower, upper = ([], [])
+    for step in range(size - 1):
+        if step % 2 == 0:
+            lower.append(lax.ppermute(lower[-1] if lower else tokens, "shard", pairs))
+        else:
+            upper.append(lax.ppermute(upper[-1] if upper else tokens, "shard", back))
+    parts = jnp.stack([*lower[::-1], tokens, *upper])
+    shift = lax.axis_index("shard") - len(lower)
+    parts = parts[(jnp.arange(size) - shift) % size]
+    gathered = laid_out(parts, 1)
     row_blocks = gathered.shape[1] // block_size
     tokens3 = gathered.reshape(token_count, row_blocks, block_size)
     gate_in = jnp.take(tokens3, gate_rows, axis=1)

time: 283 us -> 300 us (1.060)
  starting transfers between devices: 15.3 us -> 40.1 us
  waiting for transfers between devices: 141 us -> 126 us
  local copies, waits for them, and re-layouts: 54.1 us -> 57.4 us
    all_gather x1 -> x0, waiting for transfers between devices: 68.2 us -> none  [body(): gathered = lax.all_gather(tokens, 'shard', axis=1, tiled=True)]
    ppermute x0 -> x3, waiting for transfers between devices: none -> 54.7 us  [the longest x2 54.7 us: body(): lower.append(lax.ppermute(lower[-1] if lower else tokens, 'shard', pairs))]
    ppermute x0 -> x3, starting transfers between devices: none -> 22.6 us  [the longest x2 20.8 us: body(): lower.append(lax.ppermute(lower[-1] if lower else tokens, 'shard', pairs))]
    transpose x0 -> x1, local copies, waits for them, and re-layouts: none -> 3.93 us  [laid_out(): return jnp.moveaxis(blocks, 0, dim).reshape(dims)]
    another operation x0 -> x1, local copies, waits for them, and re-layouts: none -> 3.21 us  [body(): tokens3 = gathered.reshape(token_count, row_blocks, block_size)]
    reshape x1 -> x0, local copies, waits for them, and re-layouts: 3.21 us -> none  [body(): tokens3 = gathered.reshape(token_count, row_blocks, block_size)]
    unnamed x46 -> x49, local copies, waits for them, and re-layouts: 12 us -> 9.4 us
    unnamed x3 -> x2, waiting for transfers between devices: 68.1 us -> 68.2 us
  transfers between devices with their start and end apart: 5 -> 7, of which waited for: 3 -> 4; matrix products, arithmetic and copies ran while one was open for 34% -> 32% of each run, Pallas kernels for 0% -> 0%
where the time goes in v1:
time: 300 us; the launch traced here: 299 us
  waiting for transfers between devices  126 us (42%)
  local copies, waits for them, and re-layouts  57.4 us (19%)
  starting transfers between devices  40.1 us (13%)
  other arithmetic  35.4 us (12%)
  matrix products  24.8 us (8%)
  between operations  14.9 us (5%)
    unnamed x2, waiting for transfers between devices  68.2 us
    ppermute x2, waiting for transfers between devices, body(): lower.append(lax.ppermute(lower[-1] if lower else tokens, 'shard', pairs))  54.7 us
    ppermute x2, starting transfers between devices, body(): lower.append(lax.ppermute(lower[-1] if lower else tokens, 'shard', pairs))  20.8 us
    scatter-add x2, other arithmetic, body(): input_terms = input_terms.at[:, column_ids, gate_rows].add(back_gate).at[...  20.6 us
    unnamed x49, local copies, waits for them, and re-layouts  9.4 us
    all_to_all x1, starting transfers between devices, body(): lax.all_to_all(outgoing, 'shard', split_axis=1, concat_axis=1, tiled=True)  6.49 us
    convert_element_type x1, local copies, waits for them, and re-layouts, body(): input_terms.astype(jnp.bfloat16)  6.39 us
    gather x2, local copies, waits for them, and re-layouts, body(): up_in = jnp.take(tokens3, up_rows, axis=1)  6.16 us
  transfers between devices with their start and end apart: 7, of which 4 were waited for; matrix products, arithmetic and copies ran while one was open for 32% of the time, Pallas kernels for 0%

profile of v1, /device:TPU:0, one launch (start us, length us, event | category | flops | bytes accessed | tf_op | source)
XLA Modules:
  0.0 298.5 jit_solution(7360687809434688846)
XLA Ops:
  11.9 3.3 %copy.66 = bf16[256,32,128]{0,2,1:T(8,128)(2,1)S(1)} copy(bf16[256,32,128]{2,0,1:T(8,128)(2,1)} %bitcast.159) | data formatting | bytes 4194304 | tf_op jit(solution)/shard_map/jit(_take)/gather | solution.py:61
  17.0 6.5 %all-to-all-start.1 = ((bf16[256,4,1024]{0,2,1:T(8,128)(2,1)}), bf16[256,4,1024]{0,2,1:T(8,128)(2,1)}, u32[]{:S(2)}, u32[]{:S(2)}) async-start(bf16[256,4,1024]{0,2,1:T(8,128)(2,1)} %bitcast_select_fusion), calls=%async_computation.1 | async-start | bytes 4194304 | tf_op jit(solution)/shard_map/all_to_all | solution.py:63
  28.8 45.2 %collective-permute-done = bf16[256,1024]{1,0:T(8,128)(2,1)S(1)} collective-permute-done((bf16[256,1024]{1,0:T(8,128)(2,1)S(1)}, bf16[256,1024]{1,0:T(8,128)(2,1)S(1)}, u32[]{:S(2)}, u32[]{:S(2)}) %collective-permute-start) | collective-permute-done | bytes 524320 | tf_op jit(solution)/shard_map/ppermute | solution.py:29
  74.0 18.8 %collective-permute-start.1 = (bf16[256,1024]{1,0:T(8,128)(2,1)S(1)}, bf16[256,1024]{1,0:T(8,128)(2,1)S(1)}, u32[]{:S(2)}, u32[]{:S(2)}) collective-permute-start(bf16[256,1024]{1,0:T(8,128)(2,1)S(1)} %collective-permute-done), channel_id=1, source_target_pairs={{0,4},{4,8},{8,12},{12,0},{1,5},{5,9},{9,13},{13,1},{2,6},{6,10},{... | collective-permute-start | bytes 1572872 | tf_op jit(solution)/shard_map/ppermute | solution.py:29
  93.3 9.5 %collective-permute-done.1 = bf16[256,1024]{1,0:T(8,128)(2,1)S(1)} collective-permute-done((bf16[256,1024]{1,0:T(8,128)(2,1)S(1)}, bf16[256,1024]{1,0:T(8,128)(2,1)S(1)}, u32[]{:S(2)}, u32[]{:S(2)}) %collective-permute-start.1) | collective-permute-done | bytes 524320 | tf_op jit(solution)/shard_map/ppermute | solution.py:29
  106.4 3.9 %copy.53 = bf16[256,4,1024]{0,2,1:T(8,128)(2,1)} copy(bf16[256,4,1024]{2,0,1:T(8,128)(2,1)} %bitcast.160) | data formatting | bytes 4194304 | tf_op jit(solution)/shard_map/transpose | solution.py:10
  110.4 3.2 %copy.54 = bf16[256,32,128]{2,0,1:T(8,128)(2,1)S(1)} copy(bf16[256,32,128]{0,2,1:T(8,128)(2,1)} %bitcast.161) | data formatting | bytes 4194304 | tf_op jit(solution)/shard_map/reshape;reshape | solution.py:37
  115.7 3.9 %copy.55 = bf16[2,16,256,128]{2,3,1,0:T(8,128)(2,1)} copy(bf16[2,16,256,128]{3,2,1,0:T(8,128)(2,1)} %bitcast.157) | data formatting | bytes 4194304 | tf_op jit(solution)/shard_map/jit(_take)/gather | solution.py:38
  121.8 4.0 %copy.58 = bf16[2,16,256,128]{2,3,1,0:T(8,128)(2,1)} copy(bf16[2,16,256,128]{3,2,1,0:T(8,128)(2,1)} %bitcast.156) | data formatting | bytes 4194304 | tf_op jit(solution)/shard_map/jit(_take)/gather | solution.py:39
  125.8 3.4 %fusion.20 = f32[256,2,128]{2,0,1:T(8,128)} fusion(bf16[2,16,128,128]{3,2,1,0:T(8,128)(2,1)S(1)} %copy-done.8, bf16[2,16,256,128]{2,3,1,0:T(8,128)(2,1)} %copy.55, pred[2,16]{1,0:T(4,128)(4,1)S(1)} %compare_and_fusion.1), kind=kOutput, calls=%fused_computation.26 | convolution fusion | flops 269484032 | bytes 3407904 | tf_op jit(solution)/shard_map/nckb,ckbh->nch/dot_general | solution.py:40
  135.7 5.8 %all-to-all-start = ((bf16[256,2,4,512]{0,3,1,2:T(8,128)(2,1)}), bf16[256,2,4,512]{0,3,1,2:T(8,128)(2,1)S(1)}, u32[]{:S(2)}, u32[]{:S(2)}) async-start(bf16[256,2,4,512]{0,3,1,2:T(8,128)(2,1)} %copy.61), calls=%async_computation | async-start | bytes 4194304 | tf_op jit(solution)/shard_map/all_to_all | solution.py:47
  142.9 3.9 %fusion.35 = f32[2,256,16,128]{3,1,2,0:T(8,128)} fusion(bf16[2,16,128,128]{3,2,1,0:T(8,128)(2,1)} %param.11, bf16[256,2,128]{2,0,1:T(8,128)(2,1)S(1)} %get-tuple-element.15), kind=kOutput, calls=%fused_computation.42 | convolution fusion | flops 268435456 | bytes 5373952 | tf_op jit(solution)/shard_map/nch,ckbh->nckb/dot_general | solution.py:75
  146.8 4.3 %broadcast_in_dim.46 = f32[256,2,32,128]{3,0,2,1:T(8,128)} broadcast(f32[]{:T(128)} %constant.65.clone.1), dimensions={} | broadcast | bytes 8388612 | tf_op jit(solution)/shard_map/broadcast_in_dim | solution.py:80
  151.1 10.3 %scatter_fusion = f32[256,2,32,128]{3,0,2,1:T(8,128)} fusion(f32[256,2,32,128]{3,0,2,1:T(8,128)} %broadcast_in_dim.46, s32[32]{0:T(128)S(1)} %reshape.171, f32[32,256,128]{2,1,0:T(8,128)} %bitcast.150), kind=kCustom, calls=%fused_computation.4 | custom fusion | flops 1048576 | bytes 12583168 | tf_op jit(solution)/shard_map/scatter-add | solution.py:83
  164.1 10.3 %scatter_fusion.1 = f32[256,2,32,128]{3,0,2,1:T(8,128)} fusion(f32[256,2,32,128]{3,0,2,1:T(8,128)} %scatter_fusion, s32[32]{0:T(128)S(1)} %reshape.177, f32[32,256,128]{2,1,0:T(8,128)} %bitcast.151), kind=kCustom, calls=%fused_computation.5 | custom fusion | flops 1048576 | bytes 12583168 | tf_op jit(solution)/shard_map/scatter-add | solution.py:85
  174.4 6.1 %convert_element_type.59 = bf16[256,2,32,128]{3,0,2,1:T(8,128)(2,1)} convert(f32[256,2,32,128]{3,0,2,1:T(8,128)} %scatter_fusion.1) | non-fusion elementwise | flops 2097152 | bytes 12582912 | tf_op jit(solution)/shard_map/convert_element_type | solution.py:87
  180.5 6.4 %copy.69 = bf16[256,2,32,128]{0,3,2,1:T(8,128)(2,1)} copy(bf16[256,2,32,128]{3,0,2,1:T(8,128)(2,1)} %convert_element_type.59) | data formatting | bytes 8388608 | tf_op jit(solution)/shard_map/convert_element_type | solution.py:87
  186.9 4.4 %copy.70 = bf16[256,2,4,1024]{0,3,1,2:T(8,128)(2,1)} copy(bf16[256,2,4,1024]{0,3,2,1:T(8,128)(2,1)} %bitcast.153) | data formatting | bytes 8388608 | tf_op jit(solution)/shard_map/reshape | solution.py:87
  191.3 5.2 %all-to-all-start.2 = ((bf16[256,2,4,1024]{0,3,1,2:T(8,128)(2,1)}), bf16[256,2,4,1024]{0,3,1,2:T(8,128)(2,1)}, u32[]{:S(2)}, u32[]{:S(2)}) async-start(bf16[256,2,4,1024]{0,3,1,2:T(8,128)(2,1)} %copy.70), calls=%async_computation.2 | async-start | bytes 8388608 | tf_op jit(solution)/shard_map/all_to_all | solution.py:90
  196.5 3.6 %fusion.16 = bf16[2,128,4,4,128]{4,1,3,2,0:T(8,128)(2,1)} fusion(bf16[256,4,2,4,128]{0,4,3,2,1:T(8,128)(2,1)} %bitcast.35, bf16[256,2,128]{2,0,1:T(8,128)(2,1)S(1)} %get-tuple-element.16), kind=kOutput, calls=%fused_computation.22 | convolution fusion | flops 268959744 | bytes 3276800 | tf_op jit(solution)/shard_map/nocjb,nch->cojhb/dot_general | solution.py:94
  205.6 68.2 %all-reduce.6.cloned.1.call-done = (bf16[2,16,128,128]{3,2,1,0:T(8,128)(2,1)}, bf16[2,16,128,128]{3,2,1,0:T(8,128)(2,1)}, bf16[2,16,128,128]{3,2,1,0:T(8,128)(2,1)}) async-done(((bf16[2,16,128,128]{3,2,1,0:T(8,128)(2,1)}, bf16[2,16,128,128]{3,2,1,0:T(8,128)(2,1)}, bf16[2,16,128,128]{3,2,1,0:T(8,128)(2,1)}), (bf16[2,16,128,128]{3,2,1,0:T(8,128)(2,1)}, bf16[2,16,128,128]{3,2,1,0:T(8,128)(2,1)}, ...) | async-done | bytes 3145744
  277.3 3.2 %copy.63 = bf16[256,2,4,4,128]{4,2,3,0,1:T(4,128)(2,1)} copy(bf16[256,2,4,4,128]{0,4,3,1,2:T(8,128)(2,1)S(1)} %bitcast.158) | data formatting | bytes 4194304 | tf_op jit(solution)/shard_map/reshape | solution.py:48
  280.5 3.2 %fusion.19 = bf16[8,256,128]{2,0,1:T(8,128)(2,1)S(1)} fusion(bf16[256,2,4,4,128]{4,2,3,0,1:T(4,128)(2,1)} %copy.63, s32[4,2,4]{0,2,1:T(4,128)S(1)} %copy.52), kind=kOutput, calls=%fused_computation.24 | convolution fusion | flops 17039616 | bytes 2621568 | tf_op jit(solution)/shard_map/ncsjb,scjr->nrb/dot_general | solution.py:56
  287.6 3.0 %reduce_sum.12 = bf16[256,1024]{0,1:T(8,128)(2,1)S(1)} reduce(bf16[256,2,4,1024]{0,3,1,2:T(8,128)(2,1)} %all-to-all-done.2, bf16[]{:T(256)} %constant.69.clone.1), dimensions={1,2}, to_apply=%region_2.4 | reduce | flops 1835008 | bytes 4718594 | tf_op jit(solution)/shard_map/reduce_sum | solution.py:91
  (93 shorter events, 43.9 us)
Async XLA Ops:
  7.2 124.8 %copy-start = (bf16[2,16,128,128]{3,2,1,0:T(8,128)(2,1)S(1)}, bf16[2,16,128,128]{3,2,1,0:T(8,128)(2,1)}, u32[]{:S(2)}) copy-start(bf16[2,16,128,128]{3,2,1,0:T(8,128)(2,1)} %param.12) | copy-start | bytes 3145732
  17.0 6.5 %copy-start.9 = (bf16[256,1024]{1,0:T(8,128)(2,1)S(1)}, bf16[256,1024]{1,0:T(8,128)(2,1)}, u32[]{:S(2)}) copy-start(bf16[256,1024]{1,0:T(8,128)(2,1)} %param.10) | copy-start | bytes 1572868
  17.0 10.3 %copy-start.11 = (s32[2,16]{1,0:T(2,128)S(1)}, s32[2,16]{1,0:T(2,128)}, u32[]{:S(2)}) copy-start(s32[2,16]{1,0:T(2,128)} %param.14) | copy-start | bytes 388
  17.0 10.4 %copy-start.12 = (s32[2,16]{1,0:T(2,128)S(1)}, s32[2,16]{1,0:T(2,128)}, u32[]{:S(2)}) copy-start(s32[2,16]{1,0:T(2,128)} %param.15) | copy-start | bytes 388
  17.0 10.5 %copy-start.2 = (bf16[2,16,128,128]{3,2,1,0:T(8,128)(2,1)S(1)}, bf16[2,16,128,128]{3,2,1,0:T(8,128)(2,1)}, u32[]{:S(2)}) copy-start(bf16[2,16,128,128]{3,2,1,0:T(8,128)(2,1)} %param.13) | copy-start | bytes 3145732
  17.0 112.3 %all-to-all-start.1 = ((bf16[256,4,1024]{0,2,1:T(8,128)(2,1)}), bf16[256,4,1024]{0,2,1:T(8,128)(2,1)}, u32[]{:S(2)}, u32[]{:S(2)}) async-start(bf16[256,4,1024]{0,2,1:T(8,128)(2,1)} %bitcast_select_fusion), calls=%async_computation.1 | async-start | bytes 4194304 | tf_op jit(solution)/shard_map/all_to_all | solution.py:63
  23.5 50.5 %collective-permute-start = (bf16[256,1024]{1,0:T(8,128)(2,1)S(1)}, bf16[256,1024]{1,0:T(8,128)(2,1)S(1)}, u32[]{:S(2)}, u32[]{:S(2)}) collective-permute-start(bf16[256,1024]{1,0:T(8,128)(2,1)S(1)} %copy-done.9), channel_id=1, source_target_pairs={{0,4},{4,8},{8,12},{12,0},{1,5},{5,9},{9,13},{13,1},{2,6},{6,10},{... | collective-permute-start | bytes 1572872 | tf_op jit(solution)/shard_map/ppermute | solution.py:29
  25.5 67.8 %collective-permute-start.2 = (bf16[256,1024]{1,0:T(8,128)(2,1)S(1)}, bf16[256,1024]{1,0:T(8,128)(2,1)}, u32[]{:S(2)}, u32[]{:S(2)}) collective-permute-start(bf16[256,1024]{1,0:T(8,128)(2,1)S(1)} %copy-done.9), channel_id=1, source_target_pairs={{4,0},{8,4},{12,8},{0,12},{5,1},{9,5},{13,9},{1,13},{6,2},{10,6},{... | collective-permute-start | bytes 1572872 | tf_op jit(solution)/shard_map/ppermute | solution.py:31
  74.0 28.8 %copy-start.10 = (bf16[256,1024]{1,0:T(8,128)(2,1)}, bf16[256,1024]{1,0:T(8,128)(2,1)S(1)}, u32[]{:S(2)}) copy-start(bf16[256,1024]{1,0:T(8,128)(2,1)S(1)} %collective-permute-done) | copy-start | bytes 1572868
  74.0 28.8 %collective-permute-start.1 = (bf16[256,1024]{1,0:T(8,128)(2,1)S(1)}, bf16[256,1024]{1,0:T(8,128)(2,1)S(1)}, u32[]{:S(2)}, u32[]{:S(2)}) collective-permute-start(bf16[256,1024]{1,0:T(8,128)(2,1)S(1)} %collective-permute-done), channel_id=1, source_target_pairs={{0,4},{4,8},{8,12},{12,0},{1,5},{5,9},{9,13},{13,1},{2,6},{6,10},{... | collective-permute-start | bytes 1572872 | tf_op jit(solution)/shard_map/ppermute | solution.py:29
  92.8 33.0 %copy-start.17 = (pred[2,16]{1,0:T(4,128)(4,1)}, pred[2,16]{1,0:T(4,128)(4,1)S(1)}, u32[]{:S(2)}) copy-start(pred[2,16]{1,0:T(4,128)(4,1)S(1)} %compare_and_fusion.1) | copy-start | bytes 100
  121.8 4.0 %copy-start.8 = (bf16[2,16,128,128]{3,2,1,0:T(8,128)(2,1)S(1)}, bf16[2,16,128,128]{3,2,1,0:T(8,128)(2,1)}, u32[]{:S(2)}) copy-start(bf16[2,16,128,128]{3,2,1,0:T(8,128)(2,1)} %param.11) | copy-start | bytes 3145732
  125.8 3.4 %copy-start.3 = (bf16[2,16,128,128]{3,2,1,0:T(8,128)(2,1)S(1)}, bf16[2,16,128,128]{3,2,1,0:T(8,128)(2,1)}, u32[]{:S(2)}) copy-start(bf16[2,16,128,128]{3,2,1,0:T(8,128)(2,1)} %param.13) | copy-start | bytes 3145732
  129.2 2.7 copy-start.15
  129.2 2.7 copy-start.19
  129.3 2.7 copy-start.6
  135.7 7.1 %copy-start.13 = (s32[2,16]{1,0:T(2,128)S(1)}, s32[2,16]{1,0:T(2,128)}, u32[]{:S(2)}) copy-start(s32[2,16]{1,0:T(2,128)} %param.15) | copy-start | bytes 388
  135.7 55.7 %all-to-all-start = ((bf16[256,2,4,512]{0,3,1,2:T(8,128)(2,1)}), bf16[256,2,4,512]{0,3,1,2:T(8,128)(2,1)S(1)}, u32[]{:S(2)}, u32[]{:S(2)}) async-start(bf16[256,2,4,512]{0,3,1,2:T(8,128)(2,1)} %copy.61), calls=%async_computation | async-start | bytes 4194304 | tf_op jit(solution)/shard_map/all_to_all | solution.py:47
  191.3 96.3 %all-to-all-start.2 = ((bf16[256,2,4,1024]{0,3,1,2:T(8,128)(2,1)}), bf16[256,2,4,1024]{0,3,1,2:T(8,128)(2,1)}, u32[]{:S(2)}, u32[]{:S(2)}) async-start(bf16[256,2,4,1024]{0,3,1,2:T(8,128)(2,1)} %copy.70), calls=%async_computation.2 | async-start | bytes 8388608 | tf_op jit(solution)/shard_map/all_to_all | solution.py:90
  196.5 3.6 %copy-start.18 = (pred[2,16]{1,0:T(4,128)(4,1)S(1)}, pred[2,16]{1,0:T(4,128)(4,1)}, u32[]{:S(2)}) copy-start(pred[2,16]{1,0:T(4,128)(4,1)} %copy-done.17) | copy-start | bytes 100
  196.5 77.3 %all-reduce.6.cloned.1.call-start = ((), (), s32[]{:S(2)}) async-start(), calls=%async_computation.3 | async-start | bytes 6291456
  196.5 3.6 %copy-start.5 = (bf16[2,16,256,128]{2,3,1,0:T(8,128)(2,1)S(1)}, bf16[2,16,256,128]{2,3,1,0:T(8,128)(2,1)}, u32[]{:S(2)}) copy-start(bf16[2,16,256,128]{2,3,1,0:T(8,128)(2,1)} %copy.55) | copy-start | bytes 6291460
  200.1 1.8 copy-start.16
  283.7 8.0 %copy-start.1 = (bf16[2,16,128,128]{3,2,1,0:T(8,128)(2,1)S(1)}, bf16[2,16,128,128]{3,2,1,0:T(8,128)(2,1)}, u32[]{:S(2)}) copy-start(bf16[2,16,128,128]{3,2,1,0:T(8,128)(2,1)} %param.12) | copy-start | bytes 3145732
  (3 other events, 3.6 us)
Sparse Core Ops, SparseCore 0:
  203.8 69.9 all-reduce.5
